TPU v7x, 128 devices: a whole 4x4x4 slice. The times are simulated.
128 devices in a mesh: row: 8 (over x, core), col: 16 (over z, y).
Axes of the slice: x: 4, y: 4, z: 4, core: 2. Of those that a mesh axis runs over, the one named last changes fastest.
Arguments:
- embeddings: bfloat16 [32768, 1024], P(('row', 'col')), may hold values from -6 to 6
- features: bfloat16 [32768, 256], P(('row', 'col')), may hold values from -6 to 6
- candidates: int32 [256, 38], P(('row', 'col')), may hold values from 0 to 255, as said below
Outputs:
- smoothed: bfloat16 [32768, 256], P(('row', 'col'))
Inputs may be any that keep to these rules, and one draw needn't show every extreme that they name: `candidates`: each row names 38 distinct blocks. Over the blocks held by one row of devices, the entries that name blocks held by one column of devices number at most 160, and in every row of devices some column reaches that number.
All inputs are finite; a program needn't handle non-finite values.
Results may differ from a plain program's by a relative error of at most 0.012.
The roundings to bfloat16 on the way count: a program that leaves them out, or rounds other values in their place, can miss the bound.
Values may be sent and summed in bfloat16 or wider, within the bound.
No kernel may reach another device: no remote copies, remote signals or barrier semaphores. Data moves between devices by JAX's collectives and lax.ppermute only.
A program may use at most 128 MiB of HBM per device.

v0:
```python
import jax
import jax.numpy as jnp
from jax import lax
from jax.sharding import PartitionSpec as P

EMB = 1024
FEAT = 256
BLOCK = 128
NB_DEV = 2
BETA = 16


def unit_rows(embeddings):
    values = embeddings.astype(jnp.float32)
    factor = lax.rsqrt(jnp.mean(values * values, axis=1, keepdims=True) + 1e-06) * values.shape[
        1
    ] ** (-0.5)
    return (values * factor).astype(jnp.bfloat16)


def pair_lists(keep, cand_local, query_ids, block_lists):
    query_blocks, list_len = keep.shape
    kept_int = keep.astype(jnp.int32)
    rank = jnp.cumsum(kept_int, axis=1) - 1
    destination = jnp.where(keep, rank, list_len)
    query_rows = jnp.broadcast_to(
        jnp.arange(query_blocks, dtype=jnp.int32)[:, None], (query_blocks, list_len)
    )
    same_flag = (block_lists == query_ids[:, None]).astype(jnp.int32)
    blank_table = jnp.zeros((query_blocks, list_len), jnp.int32)
    cand_sel = blank_table.at[query_rows, destination].set(cand_local, mode="drop")
    same_sel = blank_table.at[query_rows, destination].set(same_flag, mode="drop")
    counts = jnp.sum(kept_int, axis=1)
    return (cand_sel, same_sel, counts)


def smooth_tile(query_units, cand_units, cand_feats, cand_sel, same_sel, counts):
    query_blocks, block_len, _ = query_units.shape
    feat_width = cand_feats.shape[2]
    diagonal_mask = jnp.eye(block_len, dtype=jnp.bool_)

    def turn(slot, state):
        numerator, denominator = state
        cand_idx = lax.dynamic_slice_in_dim(cand_sel, slot, 1, 1)[:, 0]
        same_idx = lax.dynamic_slice_in_dim(same_sel, slot, 1, 1)[:, 0]
        active = (slot < counts).astype(jnp.float32)
        cand_blk = jnp.take(cand_units, cand_idx, axis=0)
        feat_blk = jnp.take(cand_feats, cand_idx, axis=0)
        cosine = jnp.einsum(
            "qie,qje->qij", query_units, cand_blk, preferred_element_type=jnp.float32
        )
        weight = jnp.exp(BETA * (cosine - 1.0))
        is_self = jnp.logical_and(same_idx[:, None, None] > 0, diagonal_mask[None])
        weight = jnp.where(is_self, jnp.float32(0.0), weight) * active[:, None, None]
        numerator = numerator + jnp.einsum(
            "qij,qjf->qif",
            weight.astype(jnp.bfloat16),
            feat_blk,
            preferred_element_type=jnp.float32,
        )
        denominator = denominator + jnp.sum(weight, axis=2)
        return (numerator, denominator)

    turn_count = jnp.max(counts)
    initial = (
        jnp.zeros((query_blocks, block_len, feat_width), jnp.float32),
        jnp.zeros((query_blocks, block_len), jnp.float32),
    )
    return lax.fori_loop(0, turn_count, turn, initial)


def on_device(embeddings, features, candidates):
    units = unit_rows(embeddings)
    row_index = lax.axis_index("row")
    col_index = lax.axis_index("col")
    col_count = lax.axis_size("col")
    query_flat = lax.all_gather(units, "col", axis=0, tiled=True)
    block_lists = lax.all_gather(candidates, "col", axis=0, tiled=True)
    cand_flat, feat_flat = (
        lax.all_gather(units, "row", axis=0, tiled=True),
        lax.all_gather(features, "row", axis=0, tiled=True),
    )
    query_blocks = block_lists.shape[0]
    local = jnp.arange(query_blocks, dtype=jnp.int32)
    query_ids = (row_index * col_count + local // NB_DEV) * NB_DEV + local % NB_DEV
    holder = block_lists // NB_DEV
    keep = holder % col_count == col_index
    cand_local = holder // col_count * NB_DEV + block_lists % NB_DEV
    query_units = query_flat.reshape(-1, BLOCK, EMB)
    cand_units = cand_flat.reshape(-1, BLOCK, EMB)
    cand_feats = feat_flat.reshape(-1, BLOCK, FEAT)
    cand_sel, same_sel, counts = pair_lists(keep, cand_local, query_ids, block_lists)
    numerator, denominator = smooth_tile(
        query_units, cand_units, cand_feats, cand_sel, same_sel, counts
    )
    numerator, denominator = (
        lax.psum_scatter(numerator.reshape(-1, FEAT), "col", scatter_dimension=0, tiled=True),
        lax.psum_scatter(denominator.reshape(-1), "col", scatter_dimension=0, tiled=True),
    )
    return (numerator / denominator[:, None]).astype(jnp.bfloat16)


def solution(mesh):
    in_specs = (P(("row", "col"), None), P(("row", "col"), None), P(("row", "col"), None))
    out_specs = P(("row", "col"), None)
    return jax.shard_map(
        on_device, mesh=mesh, in_specs=in_specs, out_specs=out_specs, check_vma=False
    )
```

profile of v0, /device:TPU:0, one launch (start us, length us, event | category | flops | bytes accessed | tf_op | source)
XLA Modules:
  0.0 416.3 jit_solution(14212562513498291968)
XLA Ops:
  6.5 0.7 all-gather.9.cloned.1.call-update
  7.3 1.2 fusion.15
  8.5 2.0 fusion.16
  10.6 0.7 all-gather.7.cloned.1.call-update
  11.3 25.0 %all-gather = s32[16,2,38]{2,1,0:T(2,128)S(1)} all-gather(s32[1,2,38]{2,1,0:T(2,128)} %bitcast.38), channel_id=1, replica_groups=mesh['row'=8,'col'=16] {'col'}, dimensions={0}, use_global_device_ids=true | all-gather | bytes 5168 | tf_op jit(solution)/shard_map/all_gather | solution.py:78
  36.7 0.7 multiply_reduce_fusion
  37.5 0.7 and_reduce_fusion
  38.4 6.4 %scatter_custom_fusion = s32[1216]{0:T(1024)S(1)} fusion(s32[1216]{0:T(1024)S(1)} %reshape.115, s32[1216]{0:T(1024)S(1)} %reshape.117, s32[]{:T(128)} %constant.154.clone.1), kind=kCustom, calls=%fused_computation.58 | custom fusion | bytes 4868
  45.2 6.4 %scatter_custom_fusion.1 = s32[1216]{0:T(1024)S(1)} fusion(s32[1216]{0:T(1024)S(1)} %reshape.115, s32[1216]{0:T(1024)S(1)} %reshape.123, s32[]{:T(128)} %constant.154.clone.1), kind=kCustom, calls=%fused_computation.56 | custom fusion | bytes 4868
  51.8 0.7 reduce_max.9
  52.5 15.9 %all-gather.5.cloned.1.call-done = bf16[2048,1024]{1,0:T(8,128)(2,1)} async-done(((bf16[256,1024]{1,0:T(8,128)(2,1)}), bf16[2048,1024]{1,0:T(8,128)(2,1)}) %all-gather.5.cloned.1.call-update) | async-done | bytes 4194320 | tf_op jit(solution)/shard_map/all_gather | solution.py:80
  68.4 73.1 %all-gather.7.cloned.1.call-done = bf16[4096,1024]{1,0:T(8,128)(2,1)} async-done(((bf16[256,1024]{1,0:T(8,128)(2,1)}), bf16[4096,1024]{1,0:T(8,128)(2,1)}) %all-gather.7.cloned.1.call-update) | async-done | bytes 8388624 | tf_op jit(solution)/shard_map/all_gather | solution.py:77
  141.5 2.5 broadcast_in_dim.66
  144.0 47.2 %while.15 = (s32[]{:T(128)}, f32[32,128,256]{2,1,0:T(8,128)}, f32[32,128]{1,0:T(8,128)S(1)}, s32[]{:T(128)}, s32[32,38]{0,1:T(8,128)S(1)}, /*index=5*/s32[32,38]...) while((s32[]{:T(128)}, f32[32,128,256]{2,1,0:T(8,128)}, ...), condition=%wide.region_8.9_spmd.clone, body=%wide.region_6.8_spmd.clone.sunk | while | flops 1352156416 | bytes 50435528 | solution.py:69
  144.7 7.2 %gather_fusion.1 = bf16[32,128,1024]{2,1,0:T(8,128)(2,1)} fusion(bf16[16,128,1024]{2,1,0:T(8,128)(2,1)} %get-tuple-element.324, s32[1024]{0:T(1024)S(1)} %pad_clamp_fusion.2), kind=kCustom, calls=%fused_computation.clone.clone.1 | custom fusion | bytes 16777344 | tf_op jit(solution)/shard_map/while/body/jit(_take)/gather | solution.py:47
  151.9 9.3 %fusion.44 = (f32[32,128]{1,0:T(8,128)S(1)}, bf16[32,128,128]{1,2,0:T(8,128)(2,1)}) fusion(f32[32]{0:T(128)S(1)} %compare_convert_fusion.3, bf16[32,128,1024]{2,1,0:T(8,128)(2,1)} %get-tuple-element.325, bf16[32,128,1024]{2,1,0:T(8,128)(2,1)} %gather_fusion.1, pred[32]{0:T(512)(128)(4,1)S(1)} %get-tuple-element.289, ...), kind=kOutput, calls=%fused_computation.70.clone.1 | convolution fusion | flops 1081602048 | bytes 17858752 | tf_op jit(solution)/shard_map/while/body/qie,qje->qij/dot_general | solution.py:49
  161.3 0.7 gather_fusion
  162.0 5.3 %convolution_add_fusion.2 = f32[32,128,256]{2,1,0:T(8,128)} fusion(f32[32,128,256]{2,1,0:T(8,128)} %get-tuple-element.306, bf16[32,128,256]{2,1,0:T(8,128)(2,1)S(1)} %gather_fusion, pred[32]{0:T(512)(128)(4,1)S(1)} %get-tuple-element.289, bf16[32,128,128]{1,2,0:T(8,128)(2,1)} %get-tuple-element.290), kind=kOutput, calls=%fused_computation.9.clone.1 | convolution fusion | flops 270532608 | bytes 11534368 | tf_op jit(solution)/shard_map/while/body/qij,qjf->qif/dot_general | solution.py:55
  168.0 7.2 %gather_fusion.1 = bf16[32,128,1024]{2,1,0:T(8,128)(2,1)} fusion(bf16[16,128,1024]{2,1,0:T(8,128)(2,1)} %get-tuple-element.324, s32[1024]{0:T(1024)S(1)} %pad_clamp_fusion.2), kind=kCustom, calls=%fused_computation.clone.clone.1 | custom fusion | bytes 16777344 | tf_op jit(solution)/shard_map/while/body/jit(_take)/gather | solution.py:47
  175.2 9.3 %fusion.44 = (f32[32,128]{1,0:T(8,128)S(1)}, bf16[32,128,128]{1,2,0:T(8,128)(2,1)}) fusion(f32[32]{0:T(128)S(1)} %compare_convert_fusion.3, bf16[32,128,1024]{2,1,0:T(8,128)(2,1)} %get-tuple-element.325, bf16[32,128,1024]{2,1,0:T(8,128)(2,1)} %gather_fusion.1, pred[32]{0:T(512)(128)(4,1)S(1)} %get-tuple-element.289, ...), kind=kOutput, calls=%fused_computation.70.clone.1 | convolution fusion | flops 1081602048 | bytes 17858752 | tf_op jit(solution)/shard_map/while/body/qie,qje->qij/dot_general | solution.py:49
  185.2 5.3 %convolution_add_fusion.2 = f32[32,128,256]{2,1,0:T(8,128)} fusion(f32[32,128,256]{2,1,0:T(8,128)} %get-tuple-element.306, bf16[32,128,256]{2,1,0:T(8,128)(2,1)S(1)} %gather_fusion, pred[32]{0:T(512)(128)(4,1)S(1)} %get-tuple-element.289, bf16[32,128,128]{1,2,0:T(8,128)(2,1)} %get-tuple-element.290), kind=kOutput, calls=%fused_computation.9.clone.1 | convolution fusion | flops 270532608 | bytes 11534368 | tf_op jit(solution)/shard_map/while/body/qij,qjf->qif/dot_general | solution.py:55
  193.1 208.2 %all-reduce = f32[4096]{0:T(1024)S(1)} all-reduce(f32[4096]{0:T(1024)S(1)} %bitcast.34), channel_id=3, replica_groups=mesh['row'=8,'col'=16] {'col'}, use_global_device_ids=true, to_apply=%region_10.11.clone | all-reduce | flops 4096 | bytes 32768
  401.4 6.7 %reduce-scatter.2.cloned.1.call-done = f32[256,256]{1,0:T(8,128)} async-done(((f32[4096,256]{1,0:T(8,128)}), f32[256,256]{1,0:T(8,128)}) %reduce-scatter.2.cloned.1.call-update) | async-done | bytes 262160 | tf_op jit(solution)/shard_map/reduce_scatter | solution.py:97
  408.1 1.7 divide_convert_fusion
  (42 shorter events, 3.3 us)
Async XLA Ops:
  6.5 46.0 %all-gather.9.cloned.1.call-start = ((), (), s32[]{:S(2)}) async-start(), calls=%async_computation.3 | async-start | bytes 1179648 | tf_op jit(solution)/shard_map/all_gather | solution.py:81
  7.3 61.2 %all-gather.5.cloned.1.call-start = ((), (), s32[]{:S(2)}) async-start(), calls=%async_computation.1 | async-start | bytes 4718592 | tf_op jit(solution)/shard_map/all_gather | solution.py:80
  10.6 131.0 %all-gather.7.cloned.1.call-start = ((), (), s32[]{:S(2)}) async-start(), calls=%async_computation.2 | async-start | bytes 8912896 | tf_op jit(solution)/shard_map/all_gather | solution.py:77
  11.3 396.8 %reduce-scatter.2.cloned.1.call-start = ((), (), s32[]{:S(2)}) async-start(), calls=%async_computation.4 | async-start | bytes 4456448 | tf_op jit(solution)/shard_map/reduce_scatter | solution.py:97
  52.5 91.5 %copy-start = (bf16[2048,256]{1,0:T(8,128)(2,1)S(1)}, bf16[2048,256]{1,0:T(8,128)(2,1)}, u32[]{:S(2)}) copy-start(bf16[2048,256]{1,0:T(8,128)(2,1)} %all-gather.9.cloned.1.call-done) | copy-start | bytes 3145732
  191.2 0.7 copy-start.1
Sparse Core Ops, SparseCore 0:
  9.0 25.6 all-gather.8
  36.5 31.9 all-gather.4
  70.6 70.8 all-gather.6
  191.4 216.6 reduce-scatter.1
where the time goes:
time: 417 us; the launch traced here: 416 us
  blocking collectives  233 us (56%)
  waiting for transfers between devices  97.1 us (23%)
  local copies, waits for them, and re-layouts  33 us (8%)
  matrix products  29.2 us (7%)
  between operations  13.9 us (3%)
  other arithmetic  7.67 us (2%)
    unnamed x1, blocking collectives  208 us
    all_gather x1, waiting for transfers between devices, on_device(): query_flat = lax.all_gather(units, 'col', axis=0, tiled=True)  73.1 us
    all_gather x1, blocking collectives, on_device(): block_lists = lax.all_gather(candidates, 'col', axis=0, tiled=True)  25 us
    dot_general x2, matrix products, turn(): jnp.einsum('qie,qje->qij', query_units, cand_blk, preferred_element_type=...  18.6 us
    all_gather x1, waiting for transfers between devices, on_device(): lax.all_gather(units, 'row', axis=0, tiled=True)  15.9 us
    unnamed x11, local copies, waits for them, and re-layouts  14.4 us
    gather x2, local copies, waits for them, and re-layouts, turn(): cand_blk = jnp.take(cand_units, cand_idx, axis=0)  14.3 us
    dot_general x2, matrix products, turn(): jnp.einsum('qij,qjf->qif', weight.astype(jnp.bfloat16), feat_blk, preferr...  10.6 us
  transfers between devices with their start and end apart: 4, of which 3 were waited for; matrix products, arithmetic and copies ran while one was open for 5% of the time, Pallas kernels for 0%

commit v1 on v0

--- a/solution.py
+++ b/solution.py
@@ -8,6 +8,13 @@
 BLOCK = 128
 NB_DEV = 2
 BETA = 16
+
+
+def all_by_exchange(block, axis, d):
+    n_dev = lax.axis_size(axis)
+    blocks = jnp.stack([block for _ in range(n_dev)])
+    blocks = lax.all_to_all(blocks, axis, split_axis=0, concat_axis=0)
+    return jnp.concatenate(blocks, axis=d)
 
 
 def unit_rows(embeddings):
@@ -77,7 +84,7 @@
     query_flat = lax.all_gather(units, "col", axis=0, tiled=True)
     block_lists = lax.all_gather(candidates, "col", axis=0, tiled=True)
     cand_flat, feat_flat = (
-        lax.all_gather(units, "row", axis=0, tiled=True),
+        all_by_exchange(units, "row", 0),
         lax.all_gather(features, "row", axis=0, tiled=True),
     )
     query_blocks = block_lists.shape[0]

time: 417 us -> 388 us (0.930)
  waiting for transfers between devices: 97.1 us -> 61 us
  starting transfers between devices: 0.12 us -> 4.76 us
    all_gather x1, waiting for transfers between devices: 73.1 us -> 39.7 us  [on_device(): query_flat = lax.all_gather(units, 'col', axis=0, tiled=True)]
    all_gather x1 -> x0, waiting for transfers between devices: 15.9 us -> none  [on_device(): lax.all_gather(units, 'row', axis=0, tiled=True)]
    all_to_all x0 -> x1, waiting for transfers between devices: none -> 13.9 us  [all_by_exchange(): blocks = lax.all_to_all(blocks, axis, split_axis=0, concat_axis=0)]
    all_to_all x0 -> x1, starting transfers between devices: none -> 4.68 us  [all_by_exchange(): blocks = lax.all_to_all(blocks, axis, split_axis=0, concat_axis=0)]
    unnamed x11 -> x17, local copies, waits for them, and re-layouts: 14.4 us -> 14.4 us
  transfers between devices with their start and end apart: 4 -> 4, of which waited for: 3 -> 3; matrix products, arithmetic and copies ran while one was open for 5% -> 6% of each run, Pallas kernels for 0% -> 0%
where the time goes in v1:
time: 388 us; the launch traced here: 387 us
  blocking collectives  233 us (60%)
  waiting for transfers between devices  61 us (16%)
  local copies, waits for them, and re-layouts  36.5 us (9%)
  matrix products  29.2 us (8%)
  between operations  13.9 us (4%)
  other arithmetic  6.35 us (2%)
  starting transfers between devices  4.76 us (1%)
    unnamed x1, blocking collectives  208 us
    all_gather x1, waiting for transfers between devices, on_device(): query_flat = lax.all_gather(units, 'col', axis=0, tiled=True)  39.7 us
    all_gather x1, blocking collectives, on_device(): block_lists = lax.all_gather(candidates, 'col', axis=0, tiled=True)  25 us
    dot_general x2, matrix products, turn(): jnp.einsum('qie,qje->qij', query_units, cand_blk, preferred_element_type=...  18.6 us
    unnamed x17, local copies, waits for them, and re-layouts  14.4 us
    gather x2, local copies, waits for them, and re-layouts, turn(): cand_blk = jnp.take(cand_units, cand_idx, axis=0)  14.3 us
    all_to_all x1, waiting for transfers between devices, all_by_exchange(): blocks = lax.all_to_all(blocks, axis, split_axis=0, concat_axis=0)  13.9 us
    dot_general x2, matrix products, turn(): jnp.einsum('qij,qjf->qif', weight.astype(jnp.bfloat16), feat_blk, preferr...  10.6 us
  transfers between devices with their start and end apart: 4, of which 3 were waited for; matrix products, arithmetic and copies ran while one was open for 6% of the time, Pallas kernels for 0%

profile of v1, /device:TPU:0, one launch (start us, length us, event | category | flops | bytes accessed | tf_op | source)
XLA Modules:
  0.0 387.2 jit_solution(436440445017216651)
XLA Ops:
  6.5 0.7 all-gather.6.cloned.1.call-update
  7.3 1.2 fusion.15
  8.5 2.0 fusion.16
  10.5 3.6 stack.2
  14.1 4.7 %all-to-all-start = ((bf16[8,256,1024]{2,1,0:T(8,128)(2,1)}), bf16[8,256,1024]{2,1,0:T(8,128)(2,1)}, u32[]{:S(2)}, u32[]{:S(2)}) async-start(bf16[8,256,1024]{2,1,0:T(8,128)(2,1)} %stack.2), calls=%async_computation | async-start | bytes 8388608 | tf_op jit(solution)/shard_map/all_to_all | solution.py:16
  18.9 25.0 %all-gather = s32[16,2,38]{2,1,0:T(2,128)S(1)} all-gather(s32[1,2,38]{2,1,0:T(2,128)S(1)} %bitcast.37), channel_id=1, replica_groups=mesh['row'=8,'col'=16] {'col'}, dimensions={0}, use_global_device_ids=true | all-gather | bytes 5168 | tf_op jit(solution)/shard_map/all_gather | solution.py:85
  44.6 6.4 %scatter_custom_fusion = s32[1216]{0:T(1024)S(1)} fusion(s32[1216]{0:T(1024)S(1)} %reshape.113, s32[1216]{0:T(1024)S(1)} %reshape.115, s32[]{:T(128)} %constant.154.clone.1), kind=kCustom, calls=%fused_computation.58 | custom fusion | bytes 4868
  51.4 6.4 %scatter_custom_fusion.1 = s32[1216]{0:T(1024)S(1)} fusion(s32[1216]{0:T(1024)S(1)} %reshape.113, s32[1216]{0:T(1024)S(1)} %reshape.121, s32[]{:T(128)} %constant.154.clone.1), kind=kCustom, calls=%fused_computation.56 | custom fusion | bytes 4868
  58.0 0.7 reduce_max.9
  58.8 13.9 %all-to-all-done = bf16[8,256,1024]{2,1,0:T(8,128)(2,1)} async-done(((bf16[8,256,1024]{2,1,0:T(8,128)(2,1)}), bf16[8,256,1024]{2,1,0:T(8,128)(2,1)}, u32[]{:S(2)}, u32[]{:S(2)}) %all-to-all-start) | async-done | bytes 4194336 | tf_op jit(solution)/shard_map/all_to_all | solution.py:16
  72.6 39.7 %all-gather.4.cloned.1.call-done = bf16[4096,1024]{1,0:T(8,128)(2,1)} async-done(((bf16[256,1024]{1,0:T(8,128)(2,1)}), bf16[4096,1024]{1,0:T(8,128)(2,1)}) %all-gather.4.cloned.1.call-update) | async-done | bytes 8388624 | tf_op jit(solution)/shard_map/all_gather | solution.py:84
  112.3 2.5 broadcast_in_dim.66
  114.8 47.2 %while.15 = (s32[]{:T(128)}, f32[32,128,256]{2,1,0:T(8,128)}, f32[32,128]{1,0:T(8,128)S(1)}, s32[]{:T(128)}, s32[32,38]{0,1:T(8,128)S(1)}, /*index=5*/s32[32,38]...) while((s32[]{:T(128)}, f32[32,128,256]{2,1,0:T(8,128)}, ...), condition=%wide.region_8.9_spmd.clone, body=%wide.region_6.8_spmd.clone.sunk | while | flops 1352156416 | bytes 50435528 | solution.py:76
  115.5 7.2 %gather_fusion.1 = bf16[32,128,1024]{2,1,0:T(8,128)(2,1)} fusion(bf16[16,128,1024]{2,1,0:T(8,128)(2,1)} %get-tuple-element.324, s32[1024]{0:T(1024)S(1)} %pad_clamp_fusion.2), kind=kCustom, calls=%fused_computation.clone.clone.1 | custom fusion | bytes 16777344 | tf_op jit(solution)/shard_map/while/body/jit(_take)/gather | solution.py:54
  122.7 9.3 %fusion.44 = (f32[32,128]{1,0:T(8,128)S(1)}, bf16[32,128,128]{1,2,0:T(8,128)(2,1)}) fusion(f32[32]{0:T(128)S(1)} %compare_convert_fusion.3, bf16[32,128,1024]{2,1,0:T(8,128)(2,1)} %get-tuple-element.325, bf16[32,128,1024]{2,1,0:T(8,128)(2,1)} %gather_fusion.1, pred[32]{0:T(512)(128)(4,1)S(1)} %get-tuple-element.289, ...), kind=kOutput, calls=%fused_computation.70.clone.1 | convolution fusion | flops 1081602048 | bytes 17858752 | tf_op jit(solution)/shard_map/while/body/qie,qje->qij/dot_general | solution.py:56
  132.0 0.7 gather_fusion
  132.7 5.3 %convolution_add_fusion.2 = f32[32,128,256]{2,1,0:T(8,128)} fusion(f32[32,128,256]{2,1,0:T(8,128)} %get-tuple-element.306, bf16[32,128,256]{2,1,0:T(8,128)(2,1)S(1)} %gather_fusion, pred[32]{0:T(512)(128)(4,1)S(1)} %get-tuple-element.289, bf16[32,128,128]{1,2,0:T(8,128)(2,1)} %get-tuple-element.290), kind=kOutput, calls=%fused_computation.9.clone.1 | convolution fusion | flops 270532608 | bytes 11534368 | tf_op jit(solution)/shard_map/while/body/qij,qjf->qif/dot_general | solution.py:62
  138.8 7.2 %gather_fusion.1 = bf16[32,128,1024]{2,1,0:T(8,128)(2,1)} fusion(bf16[16,128,1024]{2,1,0:T(8,128)(2,1)} %get-tuple-element.324, s32[1024]{0:T(1024)S(1)} %pad_clamp_fusion.2), kind=kCustom, calls=%fused_computation.clone.clone.1 | custom fusion | bytes 16777344 | tf_op jit(solution)/shard_map/while/body/jit(_take)/gather | solution.py:54
  146.0 9.3 %fusion.44 = (f32[32,128]{1,0:T(8,128)S(1)}, bf16[32,128,128]{1,2,0:T(8,128)(2,1)}) fusion(f32[32]{0:T(128)S(1)} %compare_convert_fusion.3, bf16[32,128,1024]{2,1,0:T(8,128)(2,1)} %get-tuple-element.325, bf16[32,128,1024]{2,1,0:T(8,128)(2,1)} %gather_fusion.1, pred[32]{0:T(512)(128)(4,1)S(1)} %get-tuple-element.289, ...), kind=kOutput, calls=%fused_computation.70.clone.1 | convolution fusion | flops 1081602048 | bytes 17858752 | tf_op jit(solution)/shard_map/while/body/qie,qje->qij/dot_general | solution.py:56
  155.3 0.7 gather_fusion
  156.0 5.3 %convolution_add_fusion.2 = f32[32,128,256]{2,1,0:T(8,128)} fusion(f32[32,128,256]{2,1,0:T(8,128)} %get-tuple-element.306, bf16[32,128,256]{2,1,0:T(8,128)(2,1)S(1)} %gather_fusion, pred[32]{0:T(512)(128)(4,1)S(1)} %get-tuple-element.289, bf16[32,128,128]{1,2,0:T(8,128)(2,1)} %get-tuple-element.290), kind=kOutput, calls=%fused_computation.9.clone.1 | convolution fusion | flops 270532608 | bytes 11534368 | tf_op jit(solution)/shard_map/while/body/qij,qjf->qif/dot_general | solution.py:62
  163.9 208.3 %all-reduce = f32[4096]{0:T(1024)S(1)} all-reduce(f32[4096]{0:T(1024)S(1)} %bitcast.33), channel_id=3, replica_groups=mesh['row'=8,'col'=16] {'col'}, use_global_device_ids=true, to_apply=%region_10.11.clone | all-reduce | flops 4096 | bytes 32768
  372.3 6.7 %reduce-scatter.2.cloned.1.call-done = f32[256,256]{1,0:T(8,128)} async-done(((f32[4096,256]{1,0:T(8,128)}), f32[256,256]{1,0:T(8,128)}) %reduce-scatter.2.cloned.1.call-update) | async-done | bytes 262160 | tf_op jit(solution)/shard_map/reduce_scatter | solution.py:104
  378.9 1.7 divide_convert_fusion
  (48 shorter events, 2.8 us)
Async XLA Ops:
  6.5 52.2 %all-gather.6.cloned.1.call-start = ((), (), s32[]{:S(2)}) async-start(), calls=%async_computation.3 | async-start | bytes 1179648 | tf_op jit(solution)/shard_map/all_gather | solution.py:88
  7.3 105.1 %all-gather.4.cloned.1.call-start = ((), (), s32[]{:S(2)}) async-start(), calls=%async_computation.2 | async-start | bytes 8912896 | tf_op jit(solution)/shard_map/all_gather | solution.py:84
  14.1 4.8 %copy-start.1 = (s32[2,38]{1,0:T(2,128)S(1)}, s32[2,38]{1,0:T(2,128)}, u32[]{:S(2)}) copy-start(s32[2,38]{1,0:T(2,128)} %param.7) | copy-start | bytes 916
  14.1 30.1 %copy-start.3 = (s32[2]{0:T(128)S(1)}, s32[2]{0:T(128)}, u32[]{:S(2)}) copy-start(s32[2]{0:T(128)} %constant.171) | copy-start | bytes 28
  14.1 30.2 %copy-start.2 = (s32[2]{0:T(128)S(1)}, s32[2]{0:T(128)}, u32[]{:S(2)}) copy-start(s32[2]{0:T(128)} %constant.174) | copy-start | bytes 28
  14.1 58.5 %all-to-all-start = ((bf16[8,256,1024]{2,1,0:T(8,128)(2,1)}), bf16[8,256,1024]{2,1,0:T(8,128)(2,1)}, u32[]{:S(2)}, u32[]{:S(2)}) async-start(bf16[8,256,1024]{2,1,0:T(8,128)(2,1)} %stack.2), calls=%async_computation | async-start | bytes 8388608 | tf_op jit(solution)/shard_map/all_to_all | solution.py:16
  18.8 360.1 %reduce-scatter.2.cloned.1.call-start = ((), (), s32[]{:S(2)}) async-start(), calls=%async_computation.4 | async-start | bytes 4456448 | tf_op jit(solution)/shard_map/reduce_scatter | solution.py:104
  58.7 56.0 %copy-start = (bf16[2048,256]{1,0:T(8,128)(2,1)S(1)}, bf16[2048,256]{1,0:T(8,128)(2,1)}, u32[]{:S(2)}) copy-start(bf16[2048,256]{1,0:T(8,128)(2,1)} %all-gather.6.cloned.1.call-done) | copy-start | bytes 3145732
  162.0 0.7 copy-start.4
Sparse Core Ops, SparseCore 0:
  9.0 29.8 all-gather.5
  41.1 71.1 all-gather.3
  162.1 216.7 reduce-scatter.1
